TPU v7x, 32 devices: a whole 2x2x4 slice. The times are simulated.
32 devices in a mesh: dp: 16 (over z, y, x), sub: 2 (over core).
Axes of the slice: x: 2, y: 2, z: 4, core: 2. Of those that a mesh axis runs over, the one named last changes fastest.
Arguments:
- points: bfloat16 [16384, 256], P(('dp', 'sub'))
- candidates: int32 [4, 768], replicated, may hold values from 0 to 16383, as said below
- owner_slot: int32 [3072], replicated, may hold values from 0 to 3071, each once
Outputs:
- centroids: float32 [3072, 256], P(('dp', 'sub'))
- masses: float32 [3072], P(('dp', 'sub'))
- min_dist: float32 [16384], P(('dp', 'sub'))
Inputs may be any that keep to these rules, and one draw needn't show every extreme that they name: In each round the candidates are distinct rows; no device's block of 512 rows holds more than 96 candidates of one round, and in each round some device's block holds exactly 96.
All inputs are finite; a program needn't handle non-finite values.
Results may differ from a plain program's by a relative error of at most 0.00055.
Values may be sent and summed in bfloat16 or wider, within the bound.
No kernel may reach another device: no remote copies, remote signals or barrier semaphores. Data moves between devices by JAX's collectives and lax.ppermute only.
A program may use at most 64 MiB of HBM per device.

v0:
```python
import jax
import jax.numpy as jnp
from jax import lax
from jax.sharding import PartitionSpec as P


def pick_rows(round_rows, points, my_device):
    row_count = points.shape[0]
    flat_rows = round_rows.reshape(-1)
    owner_dev = flat_rows // row_count
    local_row = flat_rows % row_count
    mine = owner_dev == my_device
    picked = jnp.where(
        mine[:, None], points[local_row].astype(jnp.float32), jnp.zeros((), jnp.float32)
    )
    return lax.psum(picked, ("dp", "sub")).astype(jnp.bfloat16)


def on_device(points, candidates, owner_slot):
    row_count = points.shape[0]
    width_dim = points.shape[1]
    round_count = candidates.shape[0]
    cand_count = candidates.shape[1]
    my_device = lax.axis_index(("dp", "sub"))
    block_rows = min(512, row_count)
    point_norm = jnp.sum(points.astype(jnp.float32) ** 2, axis=1)
    all_chosen = pick_rows(candidates, points, my_device)
    chosen_list = [
        all_chosen[which_round * cand_count : (which_round + 1) * cand_count]
        for which_round in range(round_count)
    ]
    nearest_parts = [jnp.full((block_rows,), 3e38, jnp.float32)]
    sums_parts = []
    mass_parts = []
    for which_round in range(round_count):
        chosen = chosen_list[which_round]
        cand_norm = jnp.sum(chosen.astype(jnp.float32) ** 2, axis=1)
        dots = lax.dot_general(
            points, chosen, (((1,), (1,)), ((), ())), preferred_element_type=jnp.float32
        )
        dist = point_norm[:, None] + cand_norm[None, :] - 2.0 * dots
        nearest_parts[0] = jnp.minimum(nearest_parts[0], jnp.min(dist, axis=1))
        kernel = jnp.exp(-dist / 0.25).astype(jnp.bfloat16)
        sums_round = lax.dot_general(
            kernel, points, (((0,), (0,)), ((), ())), preferred_element_type=jnp.float32
        )
        mass_round = jnp.sum(kernel.astype(jnp.float32), axis=0)
        sums_parts.append(sums_round)
        mass_parts.append(mass_round)
    partial_sums = jnp.concatenate(sums_parts, axis=0)
    partial_mass = jnp.concatenate(mass_parts, axis=0)
    total_rows = partial_sums.shape[0]
    placed_sums = jnp.zeros((total_rows, width_dim), jnp.float32).at[owner_slot].set(partial_sums)
    placed_mass = jnp.zeros((total_rows,), jnp.float32).at[owner_slot].set(partial_mass)
    summed, masses = (
        lax.psum_scatter(placed_sums, ("dp", "sub"), scatter_dimension=0, tiled=True),
        lax.psum_scatter(placed_mass, ("dp", "sub"), scatter_dimension=0, tiled=True),
    )
    centroids = summed / masses[:, None]
    min_dist = nearest_parts[0]
    return (centroids, masses, min_dist)


def solution(mesh):
    placed = (P(("dp", "sub"), None), P(), P())
    return jax.shard_map(
        on_device,
        mesh=mesh,
        in_specs=placed,
        out_specs=(P(("dp", "sub"), None), P(("dp", "sub")), P(("dp", "sub"))),
        check_vma=False,
    )
```

profile of v0, /device:TPU:0, one launch (start us, length us, event | category | flops | bytes accessed | tf_op | source)
XLA Modules:
  0.0 239.9 jit_solution(6603793152134570887)
XLA Ops:
  7.2 0.0 copy-start
  7.2 0.0 reduce-scatter.2.cloned.1.call-start
  7.2 0.7 compare_select_fusion.3
  8.0 0.7 reshape.107
  8.7 0.7 copy.6
  9.4 0.1 compare_select_fusion
  9.5 1.1 multiply_reduce_fusion.4
  10.6 0.0 copy-done
  10.6 13.0 %gather_fusion = bf16[3072,256]{1,0:T(8,128)(2,1)} fusion(bf16[512,256]{1,0:T(8,128)(2,1)S(1)} %copy-done, s32[3072]{0:T(1024)S(1)} %broadcast_clamp_fusion), kind=kCustom, calls=%fused_computation | custom fusion | bytes 3158016 | tf_op jit(solution)/shard_map/gather | solution.py:14
  23.6 2.7 %convert_select_fusion = f32[3072,256]{1,0:T(8,128)S(1)} fusion(bf16[3072,256]{1,0:T(8,128)(2,1)} %gather_fusion, pred[3072]{0:T(1024)(128)(4,1)S(1)} %fusion.18), kind=kLoop, calls=%fused_computation.11 | loop fusion | flops 1572864 | bytes 4721664 | tf_op jit(solution)/shard_map/jit(_where)/select_n | solution.py:13
  26.3 80.7 %all-reduce.2 = bf16[3072,256]{1,0:T(8,128)(2,1)} all-reduce(f32[3072,256]{1,0:T(8,128)S(1)} %convert_select_fusion), channel_id=1, replica_groups=mesh['dp'=16,'sub'=2] {'dp','sub'}, use_global_device_ids=true, to_apply=%region_1.2 | all-reduce | flops 786432 | bytes 4718592 | tf_op jit(solution)/shard_map/psum | solution.py:16
  107.0 0.0 copy-start.1
  107.0 1.9 multiply_reduce_fusion.3
  108.9 0.0 copy-done.1
  109.0 0.7 fusion.30
  109.6 0.4 fusion.16
  110.0 0.7 fusion.29
  110.7 0.4 fusion.15
  111.1 0.7 fusion.28
  111.8 0.4 fusion.14
  112.2 0.7 fusion.27
  112.9 0.4 fusion.13
  113.3 17.1 %scatter_custom_fusion = f32[3072,256]{1,0:T(8,128)} fusion(s32[3072]{0:T(1024)S(1)} %compare_select_fusion.3, f32[768,256]{1,0:T(8,128)S(1)} %fusion.16, f32[]{:T(128)} %constant.61, f32[768,256]{1,0:T(8,128)S(1)} %fusion.15, f32[768,256]{1,0:T(8,128)S(1)} %fusion.14, f32[768,256]{1,0:T(8,128)S(1)} %fusion.13, f32[]{:T(128)} %constant.43.clone.1), kind=kCustom, calls=%fused_computation.3 | custom fusion | flops 2359296 | bytes 6291464 | tf_op jit(solution)/shard_map/scatter | solution.py:53
  130.4 0.0 reduce-scatter.2.cloned.1.call-update
  130.4 11.8 %scatter_custom_fusion.1 = f32[3072]{0:T(1024)S(1)} fusion(s32[3072]{0:T(1024)S(1)} %compare_select_fusion.3, f32[3072]{0:T(1024)S(1)} %pad_maximum_fusion, f32[]{:T(128)} %constant.43.clone.1), kind=kCustom, calls=%fused_computation.55 | custom fusion | bytes 12292 | tf_op jit(solution)/shard_map/scatter | solution.py:54
  142.3 38.4 %all-reduce = f32[3072]{0:T(1024)S(1)} all-reduce(f32[3072]{0:T(1024)S(1)} %scatter_custom_fusion.1), channel_id=3, replica_groups=mesh['dp'=16,'sub'=2] {'dp','sub'}, use_global_device_ids=true, to_apply=%region_13.14.clone | all-reduce | flops 3072 | bytes 24576
  180.6 0.1 dynamic-slice
  180.7 0.0 copy-start.2
  180.7 0.6 minimum_minimum_fusion
  181.3 50.1 %reduce-scatter.2.cloned.1.call-done = f32[96,256]{1,0:T(8,128)} async-done(((f32[3072,256]{1,0:T(8,128)}), f32[96,256]{1,0:T(8,128)}) %reduce-scatter.2.cloned.1.call-update) | async-done | bytes 98320 | tf_op jit(solution)/shard_map/reduce_scatter | solution.py:56
  231.4 1.6 broadcast_divide_fusion
  233.0 0.0 copy-done.2
  (3 shorter events, 0.0 us)
Async XLA Ops:
  7.2 3.4 %copy-start = (bf16[512,256]{1,0:T(8,128)(2,1)S(1)}, bf16[512,256]{1,0:T(8,128)(2,1)}, u32[]{:S(2)}) copy-start(bf16[512,256]{1,0:T(8,128)(2,1)} %param.3) | copy-start | bytes 786436
  7.2 224.2 %reduce-scatter.2.cloned.1.call-start = ((), (), s32[]{:S(2)}) async-start(), calls=%async_computation.1 | async-start | bytes 3244032 | tf_op jit(solution)/shard_map/reduce_scatter | solution.py:56
  107.0 2.0 copy-start.1
  180.7 52.3 %copy-start.2 = (f32[96]{0:T(128)}, f32[96]{0:T(128)S(1)}, u32[]{:S(2)}) copy-start(f32[96]{0:T(128)S(1)} %dynamic-slice) | copy-start | bytes 1156
Sparse Core Ops, SparseCore 0:
  130.5 100.8 reduce-scatter.1
where the time goes:
time: 240 us
  blocking collectives  119 us (50%)
  waiting for transfers between devices  50.1 us (21%)
  local copies, waits for them, and re-layouts  26.3 us (11%)
  other arithmetic  25.9 us (11%)
  between operations  14.2 us (6%)
  matrix products  4.27 us (2%)
    psum x1, blocking collectives, pick_rows(): return lax.psum(picked, ('dp', 'sub')).astype(jnp.bfloat16)  80.7 us
    reduce_scatter x1, waiting for transfers between devices, on_device(): lax.psum_scatter(placed_sums, ('dp', 'sub'), scatter_dimension=0, tiled=T...  50.1 us
    unnamed x1, blocking collectives  38.4 us
    scatter x1, other arithmetic, on_device(): jnp.zeros((total_rows, width_dim), jnp.float32).at[owner_slot]  17.1 us
    gather x1, local copies, waits for them, and re-layouts, pick_rows(): points[local_row].astype(jnp.float32)  13 us
    scatter x1, local copies, waits for them, and re-layouts, on_device(): jnp.zeros((total_rows,), jnp.float32).at[owner_slot].set(partial_mass)  11.8 us
  transfers between devices with their start and end apart: 1, of which 1 were waited for; matrix products, arithmetic and copies ran while one was open for 5% of the time, Pallas kernels for 0%

commit v1 on v0

--- a/solution.py
+++ b/solution.py
@@ -13,7 +13,7 @@
     picked = jnp.where(
         mine[:, None], points[local_row].astype(jnp.float32), jnp.zeros((), jnp.float32)
     )
-    return lax.psum(picked, ("dp", "sub")).astype(jnp.bfloat16)
+    return lax.psum(lax.psum(picked, "sub"), "dp").astype(jnp.bfloat16)
 
 
 def on_device(points, candidates, owner_slot):

time: 240 us -> 323 us (1.35)
  blocking collectives: 119 us -> 181 us
  waiting for transfers between devices: 50.1 us -> 73.9 us
    psum x1, blocking collectives: 80.7 us -> 140 us  [pick_rows(): return lax.psum(lax.psum(picked, 'sub'), 'dp').astype(jnp.bfloat16)]
    psum x0 -> x1, waiting for transfers between devices: none -> 25.1 us  [pick_rows(): return lax.psum(lax.psum(picked, 'sub'), 'dp').astype(jnp.bfloat16)]
  transfers between devices with their start and end apart: 1 -> 2, of which waited for: 1 -> 2; matrix products, arithmetic and copies ran while one was open for 5% -> 4% of each run, Pallas kernels for 0% -> 0%
where the time goes in v1:
time: 323 us; the launch traced here: 322 us
  blocking collectives  181 us (56%)
  waiting for transfers between devices  73.9 us (23%)
  local copies, waits for them, and re-layouts  25.7 us (8%)
  other arithmetic  22.8 us (7%)
  between operations  14.2 us (4%)
  matrix products  5.12 us (2%)
    psum x1, blocking collectives, pick_rows(): return lax.psum(lax.psum(picked, 'sub'), 'dp').astype(jnp.bfloat16)  140 us
    reduce_scatter x1, waiting for transfers between devices, on_device(): lax.psum_scatter(placed_sums, ('dp', 'sub'), scatter_dimension=0, tiled=T...  48.8 us
    unnamed x1, blocking collectives  40.8 us
    psum x1, waiting for transfers between devices, pick_rows(): return lax.psum(lax.psum(picked, 'sub'), 'dp').astype(jnp.bfloat16)  25.1 us
    scatter x1, other arithmetic, on_device(): jnp.zeros((total_rows, width_dim), jnp.float32).at[owner_slot]  17.1 us
    scatter x1, local copies, waits for them, and re-layouts, on_device(): jnp.zeros((total_rows,), jnp.float32).at[owner_slot].set(partial_mass)  11.8 us
    gather x1, local copies, waits for them, and re-layouts, pick_rows(): points[local_row].astype(jnp.float32)  10.8 us
  transfers between devices with their start and end apart: 2, of which 2 were waited for; matrix products, arithmetic and copies ran while one was open for 4% of the time, Pallas kernels for 0%

profile of v1, /device:TPU:0, one launch (start us, length us, event | category | flops | bytes accessed | tf_op | source)
XLA Modules:
  0.0 322.5 jit_solution(817018153103667169)
XLA Ops:
  7.2 0.0 all-reduce.4.cloned.1.call-start
  7.2 0.7 reshape.107
  7.9 0.7 copy.6
  8.7 0.1 compare_select_fusion
  8.7 10.8 %gather_fusion = bf16[3072,256]{1,0:T(8,128)(2,1)S(1)} fusion(bf16[512,256]{1,0:T(8,128)(2,1)} %param.3, s32[3072]{0:T(1024)S(1)} %broadcast_clamp_fusion), kind=kCustom, calls=%fused_computation | custom fusion | bytes 3158016 | tf_op jit(solution)/shard_map/gather | solution.py:14
  19.6 2.8 convert_select_fusion
  22.3 0.0 all-reduce.4.cloned.1.call-update
  22.4 0.0 reduce-scatter.2.cloned.1.call-start
  22.4 0.9 copy-done
  23.3 0.1 multiply_reduce_fusion.4
  23.4 0.0 copy-done.2
  23.5 25.1 %all-reduce.4.cloned.1.call-done = f32[3072,256]{1,0:T(8,128)} async-done(((f32[3072,256]{1,0:T(8,128)}), f32[3072,256]{1,0:T(8,128)}) %all-reduce.4.cloned.1.call-update) | async-done | bytes 3145744 | tf_op jit(solution)/shard_map/psum | solution.py:16
  48.5 139.8 %all-reduce.5 = bf16[3072,256]{1,0:T(8,128)(2,1)S(1)} all-reduce(f32[3072,256]{1,0:T(8,128)} %all-reduce.4.cloned.1.call-done), channel_id=1, replica_groups=mesh['dp'=16,'sub'=2] {'dp'}, use_global_device_ids=true, to_apply=%region_2.3 | all-reduce | flops 786432 | bytes 4718592 | tf_op jit(solution)/shard_map/psum | solution.py:16
  188.4 0.5 multiply_reduce_fusion.3
  188.9 0.7 fusion.30
  189.6 0.4 fusion.16
  189.9 0.7 fusion.29
  190.6 0.4 fusion.15
  191.0 0.7 fusion.28
  191.7 1.3 fusion.14
  193.0 0.7 fusion.27
  193.6 0.0 copy-start.1
  193.7 0.4 fusion.13
  194.0 0.7 copy-done.1
  194.8 17.1 %scatter_custom_fusion = f32[3072,256]{1,0:T(8,128)} fusion(s32[3072]{0:T(1024)S(1)} %compare_select_fusion.3, f32[768,256]{1,0:T(8,128)S(1)} %fusion.16, f32[]{:T(128)} %constant.61, f32[768,256]{1,0:T(8,128)S(1)} %fusion.15, f32[768,256]{1,0:T(8,128)S(1)} %copy-done.1, f32[768,256]{1,0:T(8,128)S(1)} %fusion.13, f32[]{:T(128)} %constant.43.clone.1), kind=kCustom, calls=%fused_computation.3 | custom fusion | flops 2359296 | bytes 6291464 | tf_op jit(solution)/shard_map/scatter | solution.py:53
  211.9 0.0 reduce-scatter.2.cloned.1.call-update
  212.0 11.8 %scatter_custom_fusion.1 = f32[3072]{0:T(1024)S(1)} fusion(s32[3072]{0:T(1024)S(1)} %compare_select_fusion.3, f32[3072]{0:T(1024)S(1)} %pad_maximum_fusion, f32[]{:T(128)} %constant.43.clone.1), kind=kCustom, calls=%fused_computation.55 | custom fusion | bytes 12292 | tf_op jit(solution)/shard_map/scatter | solution.py:54
  223.8 40.8 %all-reduce = f32[3072]{0:T(1024)S(1)} all-reduce(f32[3072]{0:T(1024)S(1)} %scatter_custom_fusion.1), channel_id=3, replica_groups=mesh['dp'=16,'sub'=2] {'dp','sub'}, use_global_device_ids=true, to_apply=%region_14.15.clone | all-reduce | flops 3072 | bytes 24576
  264.6 0.1 dynamic-slice
  264.6 0.6 minimum_minimum_fusion
  265.2 48.8 %reduce-scatter.2.cloned.1.call-done = f32[96,256]{1,0:T(8,128)} async-done(((f32[3072,256]{1,0:T(8,128)}), f32[96,256]{1,0:T(8,128)}) %reduce-scatter.2.cloned.1.call-update) | async-done | bytes 98320 | tf_op jit(solution)/shard_map/reduce_scatter | solution.py:56
  314.0 1.6 broadcast_divide_fusion
  (8 shorter events, 0.0 us)
Async XLA Ops:
  7.2 41.4 %all-reduce.4.cloned.1.call-start = ((), (), s32[]{:S(2)}) async-start(), calls=%async_computation.1 | async-start | bytes 6291456 | tf_op jit(solution)/shard_map/psum | solution.py:16
  22.3 0.9 copy-start
  22.3 1.1 copy-start.2
  22.4 291.7 %reduce-scatter.2.cloned.1.call-start = ((), (), s32[]{:S(2)}) async-start(), calls=%async_computation.2 | async-start | bytes 3244032 | tf_op jit(solution)/shard_map/reduce_scatter | solution.py:56
  193.6 1.1 copy-start.1
  264.6 51.0 %copy-start.3 = (f32[96]{0:T(128)}, f32[96]{0:T(128)S(1)}, u32[]{:S(2)}) copy-start(f32[96]{0:T(128)S(1)} %dynamic-slice) | copy-start | bytes 1156
Sparse Core Ops, SparseCore 0:
  22.5 26.0 all-reduce.3
  212.1 101.9 reduce-scatter.1
